TPU v7x, 32 devices: a whole 2x2x4 slice. The times are simulated.
32 devices in a mesh: section: 4 (over z), vit: 2 (over x), dp: 4 (over y, core).
Axes of the slice: x: 2, y: 2, z: 4, core: 2. Of those that a mesh axis runs over, the one named last changes fastest.
Arguments:
- grad_llm: bfloat16 [4, 1024, 4096], P('section', ('dp', 'vit')), parts along dimension 1, may hold values from -6 to 6
- vis_slot: int32 [8, 128], P('dp'), parts along dimension 0, may hold values from 0 to 255, as said below
- image_rows: int32 [16, 2], P('dp'), parts along dimension 0, may hold values from 8 to 32, as said below
- section_layer: int32 [4], replicated, may hold values from 0 to 3, each once
- vit_in: bfloat16 [4096, 1152], P(('dp', 'section', 'vit')), parts along dimension 0, may hold values from -6 to 6
- vit_out: bfloat16 [4096, 1152], P(('dp', 'section', 'vit')), parts along dimension 0, may hold values from -6 to 6
- ln_gain: float32 [1152], replicated, may hold values from 0.5 to 1.5
- ln_bias: float32 [1152], replicated, may hold values from -3 to 3
- qkv_weight: bfloat16 [1152, 3456], P('section'), may hold values from -0.1875 to 0.1875
- proj_weight: bfloat16 [1152, 1152], P('section'), may hold values from -0.1875 to 0.1875
- merge_gain: float32 [1152], replicated, may hold values from 0.5 to 1.5
- merge_bias: float32 [1152], replicated, may hold values from -3 to 3
- fc1_weight: bfloat16 [4608, 4608], P(None, 'vit'), may hold values from -0.09375 to 0.09375
- fc1_bias: float32 [4608], P('vit'), may hold values from -3 to 3
- fc2_weight: bfloat16 [4608, 4096], P('vit'), may hold values from -0.09375 to 0.09375
Outputs:
- vit_grad: bfloat16 [4096, 1152], P(('dp', 'section', 'vit')), parts along dimension 0
There are 4 independent parts, one for each index of `dp`. A program takes and returns all parts, laid end to end along the dimension named above; an argument that names none is the same for every part. Nothing has to cross between parts.
Inputs may be any that keep to these rules, and one draw needn't show every extreme that they name: `vis_slot`: every slot number appears once. On every language-model device v, the rows d * 16 to d * 16 + 15 name 16 consecutive slots that start at a multiple of 16 inside d * 32 to d * 32 + 31, the slots of vision device d (devices numbered with the group first). `image_rows`: in every group one image has exactly 32 merged tokens. `section_layer`: A permutation; the section with value 3 holds no DeepStack layer.
All inputs are finite; a program needn't handle non-finite values.
Results may differ from a plain program's by a relative error of at most 0.02.
Values may be sent and summed in bfloat16 or wider, within the bound.
No kernel may reach another device: no remote copies, remote signals or barrier semaphores. Data moves between devices by JAX's collectives and lax.ppermute only.
A program may use at most 128 MiB of HBM per device.

v0:
```python
import jax
import jax.numpy as jnp
from jax import lax
from jax.sharding import PartitionSpec as P

HEADS = 16
LEVELS = 3
norm_eps = 1e-06


def normalize(values):
    row_mean = jnp.mean(values, axis=-1, keepdims=True)
    centered = values - row_mean
    variance = jnp.mean(centered * centered, axis=-1, keepdims=True)
    inverse = lax.rsqrt(variance + norm_eps)
    return (centered * inverse, inverse)


def normalize_back(upstream, normed_rows, inverse, gain):
    scaled = upstream * gain
    mean_scaled = jnp.mean(scaled, axis=-1, keepdims=True)
    mean_cross = jnp.mean(scaled * normed_rows, axis=-1, keepdims=True)
    return (scaled - mean_scaled - normed_rows * mean_cross) * inverse


def gelu_slope(pre_act):
    cumulative = 0.5 * (1.0 + lax.erf(pre_act * 0.7071067811865476))
    density = jnp.exp(-0.5 * pre_act * pre_act) * 0.3989422804014327
    return cumulative + pre_act * density


def local(
    grad_llm,
    vis_slot,
    image_rows,
    section_layer,
    vit_in,
    vit_out,
    ln_gain,
    ln_bias,
    qkv_weight,
    proj_weight,
    merge_gain,
    merge_bias,
    fc1_weight,
    fc1_bias,
    fc2_weight,
):
    sections = lax.axis_size("section")
    shards = lax.axis_size("vit")
    section_index = lax.axis_index("section")
    shard_index = lax.axis_index("vit")
    devices = sections * shards
    patches = vit_in.shape[0]
    slots_here = patches // 4
    run_rows = grad_llm.shape[1] // devices
    llm_width = grad_llm.shape[2]
    vit_width = vit_in.shape[1]
    head_dim = vit_width // HEADS
    device_index = section_index * shards + shard_index
    qkv_full, proj_full = (
        lax.all_gather(qkv_weight, "section", axis=0, tiled=True),
        lax.all_gather(proj_weight, "section", axis=0, tiled=True),
    )
    in_rows, in_inverse = normalize(vit_in.astype(jnp.float32))
    normed = (in_rows * ln_gain + ln_bias).astype(jnp.bfloat16)
    projected = lax.dot_general(
        qkv_full, normed, (((0,), (1,)), ((), ())), preferred_element_type=jnp.float32
    )
    projected = projected.astype(jnp.bfloat16).reshape(3, HEADS, head_dim, patches)
    section_weight = jnp.where(
        section_layer < LEVELS, (section_layer + 1).astype(jnp.float32) / LEVELS, 0.0
    )
    outgoing = grad_llm[0].reshape(devices, run_rows, llm_width)
    image_ends = jnp.cumsum(image_rows[section_index])
    out_rows, out_inverse = normalize(vit_out.astype(jnp.float32))
    merge_in = (
        (out_rows * merge_gain + merge_bias).astype(jnp.bfloat16).reshape(slots_here, 4 * vit_width)
    )
    arrived = lax.all_to_all(outgoing, ("section", "vit"), split_axis=0, concat_axis=0, tiled=True)
    arrived_f = arrived.reshape(sections, shards, run_rows, llm_width).astype(jnp.float32)
    incoming = jnp.sum(arrived_f * section_weight[:, None, None, None], axis=0)
    columns = lax.dynamic_slice_in_dim(vis_slot, device_index * run_rows, run_rows, 1)
    local_slot = (columns - device_index * slots_here).reshape(-1)
    placed = (
        jnp.zeros((slots_here, llm_width), jnp.float32)
        .at[local_slot]
        .set(incoming.reshape(-1, llm_width))
    )
    slot_position = shard_index * slots_here + jnp.arange(slots_here, dtype=jnp.int32)
    merged_grad = jnp.where((slot_position < image_ends[-1])[:, None], placed, 0.0).astype(
        jnp.bfloat16
    )
    rows_in, rows_grad = (
        lax.all_gather(merge_in, "vit", axis=0, tiled=True),
        lax.all_gather(merged_grad, "vit", axis=0, tiled=True),
    )
    pre_act = jnp.dot(rows_in, fc1_weight, preferred_element_type=jnp.float32) + fc1_bias
    hidden_grad = lax.dot_general(
        rows_grad, fc2_weight, (((1,), (1,)), ((), ())), preferred_element_type=jnp.float32
    )
    pre_grad = (hidden_grad * gelu_slope(pre_act)).astype(jnp.bfloat16)
    merge_grad = lax.psum_scatter(
        lax.dot_general(
            pre_grad, fc1_weight, (((1,), (1,)), ((), ())), preferred_element_type=jnp.float32
        ).astype(jnp.bfloat16),
        "vit",
        scatter_dimension=0,
        tiled=True,
    ).astype(jnp.float32)
    out_grad = normalize_back(
        merge_grad.reshape(patches, vit_width), out_rows, out_inverse, merge_gain
    ).astype(jnp.bfloat16)
    grad_cols = lax.dot_general(
        proj_full, out_grad, (((1,), (1,)), ((), ())), preferred_element_type=jnp.float32
    )
    grad_cols = grad_cols.astype(jnp.bfloat16).reshape(1, HEADS, head_dim, patches)
    head_inputs, head_grad = (
        lax.all_to_all(projected, "vit", split_axis=1, concat_axis=3, tiled=True),
        lax.all_to_all(grad_cols, "vit", split_axis=1, concat_axis=3, tiled=True),
    )
    length = shards * patches
    block_size = min(512, length)
    block_count = length // block_size
    slot_of = jnp.arange(length, dtype=jnp.int32) // 4
    patch_image = jnp.sum((slot_of[:, None] >= image_ends[None, :]).astype(jnp.int32), axis=1)
    patch_live = slot_of < image_ends[-1]
    score_scale = head_dim ** (-0.5)
    contract_first = (((0,), (0,)), ((), ()))

    def head_backward(query_cols, key_cols, value_cols, grad_head):

        def step(carry, block_index):
            key_acc, value_acc = carry
            first_row = block_index * block_size
            query_block = lax.dynamic_slice_in_dim(query_cols, first_row, block_size, 1)
            grad_block = lax.dynamic_slice_in_dim(grad_head, first_row, block_size, 1)
            image_block = lax.dynamic_slice_in_dim(patch_image, first_row, block_size, 0)
            live_block = lax.dynamic_slice_in_dim(patch_live, first_row, block_size, 0)
            scores = (
                lax.dot_general(
                    query_block, key_cols, contract_first, preferred_element_type=jnp.float32
                )
                * score_scale
            )
            allowed = (
                (image_block[:, None] == patch_image[None, :])
                & live_block[:, None]
                & patch_live[None, :]
            )
            exponent = jnp.where(allowed, jnp.exp(jnp.where(allowed, scores, 0.0)), 0.0)
            denominator = (
                jnp.sum(exponent, axis=1, keepdims=True)
                + 1.0
                - live_block.astype(jnp.float32)[:, None]
            )
            softmax_weights = (exponent / denominator).astype(jnp.bfloat16)
            prob_grad = lax.dot_general(
                grad_block, value_cols, contract_first, preferred_element_type=jnp.float32
            )
            weighted = softmax_weights.astype(jnp.float32)
            row_dot = jnp.sum(weighted * prob_grad, axis=1, keepdims=True)
            score_grad = (weighted * (prob_grad - row_dot) * score_scale).astype(jnp.bfloat16)
            query_grad = lax.dot_general(
                key_cols, score_grad, (((1,), (1,)), ((), ())), preferred_element_type=jnp.float32
            )
            key_acc = key_acc + lax.dot_general(
                query_block,
                score_grad,
                (((1,), (0,)), ((), ())),
                preferred_element_type=jnp.float32,
            )
            value_acc = value_acc + lax.dot_general(
                grad_block,
                softmax_weights,
                (((1,), (0,)), ((), ())),
                preferred_element_type=jnp.float32,
            )
            return ((key_acc, value_acc), query_grad.astype(jnp.bfloat16))

        empty = jnp.zeros((head_dim, length), jnp.float32)
        (key_total, value_total), query_blocks = lax.scan(
            step, (empty, empty), jnp.arange(block_count, dtype=jnp.int32)
        )
        query_total = query_blocks.transpose(1, 0, 2).reshape(head_dim, length)
        return (query_total, key_total.astype(jnp.bfloat16), value_total.astype(jnp.bfloat16))

    query_all, key_all, value_all = jax.vmap(head_backward)(
        head_inputs[0], head_inputs[1], head_inputs[2], head_grad[0]
    )
    head_result = jnp.stack([query_all, key_all, value_all])
    returned = lax.all_to_all(head_result, "vit", split_axis=3, concat_axis=1, tiled=True)
    projected_grad = returned.reshape(3 * vit_width, patches)
    normed_grad = lax.dot_general(
        projected_grad, qkv_full, (((0,), (1,)), ((), ())), preferred_element_type=jnp.float32
    )
    vit_grad = out_grad.astype(jnp.float32) + normalize_back(
        normed_grad, in_rows, in_inverse, ln_gain
    )
    return vit_grad.astype(jnp.bfloat16)


def solution(mesh):
    placed = (
        P("section", ("dp", "vit"), None),
        P("dp", None),
        P("dp", None),
        P(),
        P(("dp", "section", "vit"), None),
        P(("dp", "section", "vit"), None),
        P(),
        P(),
        P("section", None),
        P("section", None),
        P(),
        P(),
        P(None, "vit"),
        P("vit"),
        P("vit", None),
    )
    return jax.shard_map(
        local,
        mesh=mesh,
        in_specs=placed,
        out_specs=P(("dp", "section", "vit"), None),
        check_vma=False,
    )
```

profile of v0, /device:TPU:0, one launch (start us, length us, event | category | flops | bytes accessed | tf_op | source)
XLA Modules:
  0.0 350.3 jit_solution(10939154692801934895)
XLA Ops:
  7.4 7.4 %all-to-all-start = ((bf16[8,16,4096]{2,1,0:T(8,128)(2,1)}), bf16[8,16,4096]{2,1,0:T(8,128)(2,1)S(1)}, u32[]{:S(2)}, u32[]{:S(2)}) async-start(bf16[8,16,4096]{2,1,0:T(8,128)(2,1)} %bitcast.69), calls=%async_computation | async-start | bytes 2097152 | tf_op jit(solution)/shard_map/all_to_all | solution.py:80
  14.9 0.2 dynamic-slice_reduce_fusion
  15.3 0.6 slice.17
  16.0 0.2 fusion.41
  16.3 0.2 fusion.36
  16.6 0.7 add_compare_fusion
  17.3 0.2 reshape.194
  17.5 16.7 %all_gather.13 = bf16[64,4608]{1,0:T(8,128)(2,1)S(1)} all-gather(bf16[32,4608]{1,0:T(8,128)(2,1)S(1)} %reshape.194), channel_id=1, replica_groups=mesh['section'=4,'vit'=2,'dp'=4] {'vit'}, dimensions={0}, use_global_device_ids=true | all-gather | bytes 884736 | tf_op jit(solution)/shard_map/all_gather | solution.py:95
  34.2 9.1 %convolution_add_fusion = f32[64,2304]{1,0:T(8,128)S(1)} fusion(bf16[64,4608]{1,0:T(8,128)(2,1)S(1)} %all_gather.13, bf16[4608,2304]{1,0:T(8,128)(2,1)} %param.27, f32[2304]{0:T(1024)S(1)} %copy-done.7), kind=kOutput, calls=%fused_computation.6 | convolution fusion | flops 1359101952 | bytes 22422528 | tf_op jit(solution)/shard_map/dot_general | solution.py:98
  43.3 0.3 fusion.6
  43.6 1.0 scatter_custom_fusion
  44.7 7.5 %all_gather.12 = bf16[64,4096]{1,0:T(8,128)(2,1)S(1)} all-gather(bf16[32,4096]{1,0:T(8,128)(2,1)S(1)} %select_convert_fusion), channel_id=1, replica_groups=mesh['section'=4,'vit'=2,'dp'=4] {'vit'}, dimensions={0}, use_global_device_ids=true | all-gather | bytes 786432 | tf_op jit(solution)/shard_map/all_gather | solution.py:96
  52.2 20.2 %convolution_convert_fusion = bf16[64,4608]{1,0:T(8,128)(2,1)} fusion(bf16[4608,2304]{1,0:T(8,128)(2,1)} %param.27, bf16[64,4096]{1,0:T(8,128)(2,1)S(1)} %all_gather.12, bf16[2304,4096]{1,0:T(8,128)(2,1)} %param.29, f32[64,2304]{1,0:T(8,128)S(1)} %convolution_add_fusion), kind=kOutput, calls=%fused_computation.2 | convolution fusion | flops 2568683520 | bytes 41811968 | tf_op jit(solution)/shard_map/dot_general | solution.py:104
  72.4 0.5 all-gather.5.cloned.1.call-update
  73.0 0.5 all-gather.3.cloned.1.call-update
  73.5 0.7 broadcast_compare_fusion
  74.3 0.2 fusion.34
  74.6 14.3 %reduce-scatter.2.cloned.1.call-done = bf16[32,4608]{1,0:T(8,128)(2,1)} async-done(((bf16[64,4608]{1,0:T(8,128)(2,1)}), bf16[32,4608]{1,0:T(8,128)(2,1)}) %reduce-scatter.2.cloned.1.call-update) | async-done | bytes 294928 | tf_op jit(solution)/shard_map/reduce_scatter | solution.py:103
  88.9 1.1 reshape.204
  90.0 0.2 multiply_reduce_fusion
  90.3 40.3 %all-gather.5.cloned.1.call-done = bf16[1152,1152]{1,0:T(8,128)(2,1)} async-done(((bf16[288,1152]{1,0:T(8,128)(2,1)}), bf16[1152,1152]{1,0:T(8,128)(2,1)}) %all-gather.5.cloned.1.call-update) | async-done | bytes 2654224 | tf_op jit(solution)/shard_map/all_gather | solution.py:63
  130.6 2.7 fusion.3
  133.3 0.9 copy.54
  134.2 3.5 all-to-all-start.2
  137.7 135.5 %all-gather.3.cloned.1.call-done = bf16[1152,3456]{1,0:T(8,128)(2,1)} async-done(((bf16[288,3456]{1,0:T(8,128)(2,1)}), bf16[1152,3456]{1,0:T(8,128)(2,1)}) %all-gather.3.cloned.1.call-update) | async-done | bytes 7962640 | tf_op jit(solution)/shard_map/all_gather | solution.py:62
  273.2 4.7 %fusion.1 = bf16[3456,128]{0,1:T(8,128)(2,1)S(1)} fusion(bf16[1152,3456]{1,0:T(8,128)(2,1)} %all-gather.3.cloned.1.call-done, bf16[128,1152]{1,0:T(8,128)(2,1)S(1)} %copy-done.3, f32[1152]{0:T(1024)S(1)} %copy-done.8, f32[1152]{0:T(1024)S(1)} %copy-done.6, f32[128]{0:T(128)S(1)} %add_rsqrt_fusion, f32[128]{0:T(128)S(1)} %broadcast_multiply_fusion.2), kind=kOutput, calls=%fused_computation.4 | convolution fusion | flops 1020542976 | bytes 9152512 | tf_op jit(solution)/shard_map/dot_general | solution.py:67
  278.0 1.0 copy.51
  279.0 1.1 copy.52
  280.1 3.7 %all-to-all-start.1 = ((bf16[3,16,72,128]{3,2,0,1:T(8,128)(2,1)}), bf16[3,16,72,128]{3,2,0,1:T(8,128)(2,1)S(1)}, u32[]{:S(2)}, u32[]{:S(2)}) async-start(bf16[3,16,72,128]{3,2,0,1:T(8,128)(2,1)} %copy.52), calls=%async_computation.2 | async-start | bytes 1769472 | tf_op jit(solution)/shard_map/all_to_all | solution.py:119
  284.0 0.3 copy.70
  284.4 0.2 reshape.201
  284.6 11.3 %all-to-all-done.1 = bf16[3,16,72,128]{3,2,0,1:T(8,128)(2,1)S(1)} async-done(((bf16[3,16,72,128]{3,2,0,1:T(8,128)(2,1)}), bf16[3,16,72,128]{3,2,0,1:T(8,128)(2,1)S(1)}, u32[]{:S(2)}, u32[]{:S(2)}) %all-to-all-start.1) | async-done | bytes 884768 | tf_op jit(solution)/shard_map/all_to_all | solution.py:119
  295.9 0.9 copy.69
  296.8 0.6 fusion.62
  297.4 0.2 reshape.200
  297.6 0.2 squeeze.21
  297.8 0.2 squeeze.24
  298.0 0.7 fusion.63
  299.0 0.4 fusion.14
  299.4 1.9 fusion.64
  301.3 3.0 fusion.12
  304.3 3.1 fusion.13
  307.4 1.1 pad_maximum_fusion
  308.5 1.9 copy.60
  310.4 22.2 %all_to_all.50 = bf16[3,8,72,256]{2,1,0,3:T(8,128)(2,1)} all-to-all(bf16[3,8,72,256]{2,1,0,3:T(8,128)(2,1)S(1)} %copy.60), channel_id=1, replica_groups=mesh['section'=4,'vit'=2,'dp'=4] {'vit'}, dimensions={3} | all-to-all | bytes 1769472 | tf_op jit(solution)/shard_map/all_to_all | solution.py:192
  332.6 3.0 copy.66
  335.7 6.0 %fusion.61 = (f32[128]{0:T(128)S(1)}, f32[128]{0:T(128)S(1)}, f32[128,1152]{1,0:T(8,128)S(1)}) fusion(f32[128]{0:T(128)S(1)} %add_rsqrt_fusion, f32[128]{0:T(128)S(1)} %broadcast_multiply_fusion.2, bf16[128,1152]{1,0:T(8,128)(2,1)S(1)} %copy-done.3, f32[1152]{0:T(1024)S(1)} %copy-done.6, bf16[3456,128]{1,0:T(8,128)(2,1)S(1)} %bitcast.62, ...), kind=kOutput, calls=%fused_computation.103 | convolution fusion | flops 1020247808 | bytes 9738752 | tf_op jit(solution)/shard_map/dot_general | solution.py:194
  341.7 1.1 fusion.33
  (51 shorter events, 1.5 us)
Async XLA Ops:
  7.4 7.5 %copy-start = (s32[4,2]{0,1:T(2,128)S(1)}, s32[4,2]{0,1:T(2,128)}, u32[]{:S(2)}) copy-start(s32[4,2]{0,1:T(2,128)} %param.17) | copy-start | bytes 100
  7.4 8.5 %copy-start.2 = (bf16[128,1152]{1,0:T(8,128)(2,1)S(1)}, bf16[128,1152]{1,0:T(8,128)(2,1)}, u32[]{:S(2)}) copy-start(bf16[128,1152]{1,0:T(8,128)(2,1)} %param.20) | copy-start | bytes 884740
  7.4 8.8 %copy-start.10 = (s32[2,128]{1,0:T(2,128)S(1)}, s32[2,128]{1,0:T(2,128)}, u32[]{:S(2)}) copy-start(s32[2,128]{1,0:T(2,128)} %param.16) | copy-start | bytes 3076
  7.4 8.9 %copy-start.9 = (f32[1152]{0:T(1024)S(1)}, f32[1152]{0:T(1024)}, u32[]{:S(2)}) copy-start(f32[1152]{0:T(1024)} %param.26) | copy-start | bytes 13828
  7.4 8.9 %copy-start.5 = (f32[1152]{0:T(1024)S(1)}, f32[1152]{0:T(1024)}, u32[]{:S(2)}) copy-start(f32[1152]{0:T(1024)} %param.25) | copy-start | bytes 13828
  7.4 26.8 %copy-start.11 = (s32[4]{0:T(128)S(1)}, s32[4]{0:T(128)}, u32[]{:S(2)}) copy-start(s32[4]{0:T(128)} %param.18) | copy-start | bytes 52
  7.4 26.8 %copy-start.7 = (f32[2304]{0:T(1024)S(1)}, f32[2304]{0:T(1024)}, u32[]{:S(2)}) copy-start(f32[2304]{0:T(1024)} %param.28) | copy-start | bytes 27652
  7.4 35.8 %all-to-all-start = ((bf16[8,16,4096]{2,1,0:T(8,128)(2,1)}), bf16[8,16,4096]{2,1,0:T(8,128)(2,1)S(1)}, u32[]{:S(2)}, u32[]{:S(2)}) async-start(bf16[8,16,4096]{2,1,0:T(8,128)(2,1)} %bitcast.69), calls=%async_computation | async-start | bytes 2097152 | tf_op jit(solution)/shard_map/all_to_all | solution.py:80
  14.8 74.0 %reduce-scatter.2.cloned.1.call-start = ((), (), s32[]{:S(2)}) async-start(), calls=%async_computation.5 | async-start | bytes 884736 | tf_op jit(solution)/shard_map/reduce_scatter | solution.py:103
  72.3 1.9 copy-start.3
  72.4 58.2 %all-gather.5.cloned.1.call-start = ((), (), s32[]{:S(2)}) async-start(), calls=%async_computation.7 | async-start | bytes 3317760 | tf_op jit(solution)/shard_map/all_gather | solution.py:63
  72.9 200.3 %all-gather.3.cloned.1.call-start = ((), (), s32[]{:S(2)}) async-start(), calls=%async_computation.6 | async-start | bytes 9953280 | tf_op jit(solution)/shard_map/all_gather | solution.py:62
  130.6 142.6 %copy-start.6 = (f32[1152]{0:T(1024)S(1)}, f32[1152]{0:T(1024)}, u32[]{:S(2)}) copy-start(f32[1152]{0:T(1024)} %param.21) | copy-start | bytes 13828
  130.6 142.6 %copy-start.8 = (f32[1152]{0:T(1024)S(1)}, f32[1152]{0:T(1024)}, u32[]{:S(2)}) copy-start(f32[1152]{0:T(1024)} %param.22) | copy-start | bytes 13828
  134.2 145.8 %all-to-all-start.2 = ((bf16[1,16,72,128]{3,2,0,1:T(8,128)(2,1)}), bf16[1,16,72,128]{3,2,0,1:T(8,128)(2,1)S(1)}, u32[]{:S(2)}, u32[]{:S(2)}) async-start(bf16[1,16,72,128]{3,2,0,1:T(8,128)(2,1)} %bitcast.12), calls=%async_computation.3 | async-start | bytes 589824 | tf_op jit(solution)/shard_map/all_to_all | solution.py:120
  280.1 15.8 %all-to-all-start.1 = ((bf16[3,16,72,128]{3,2,0,1:T(8,128)(2,1)}), bf16[3,16,72,128]{3,2,0,1:T(8,128)(2,1)S(1)}, u32[]{:S(2)}, u32[]{:S(2)}) async-start(bf16[3,16,72,128]{3,2,0,1:T(8,128)(2,1)} %copy.52), calls=%async_computation.2 | async-start | bytes 1769472 | tf_op jit(solution)/shard_map/all_to_all | solution.py:119
  297.8 0.9 copy-start.4
  335.7 7.2 %copy-start.1 = (s32[4,2]{0,1:T(2,128)S(1)}, s32[4,2]{0,1:T(2,128)}, u32[]{:S(2)}) copy-start(s32[4,2]{0,1:T(2,128)} %param.17) | copy-start | bytes 100
Sparse Core Ops, SparseCore 0:
  72.5 16.3 reduce-scatter.1
Sparse Core Ops, SparseCore 1:
  74.4 56.1 all-gather.4
  132.1 141.1 all-gather.2
where the time goes:
time: 351 us; the launch traced here: 350 us
  waiting for transfers between devices  203 us (58%)
  matrix products  51.8 us (15%)
  blocking collectives  46.3 us (13%)
  between operations  15.2 us (4%)
  starting transfers between devices  14.8 us (4%)
  local copies, waits for them, and re-layouts  13.8 us (4%)
  other arithmetic  5.89 us (2%)
    all_gather x1, waiting for transfers between devices, local(): lax.all_gather(qkv_weight, 'section', axis=0, tiled=True)  136 us
    all_gather x1, waiting for transfers between devices, local(): lax.all_gather(proj_weight, 'section', axis=0, tiled=True)  40.3 us
    all_to_all x1, blocking collectives, local(): lax.all_to_all(head_result, 'vit', split_axis=3, concat_axis=1, tiled=True)  22.2 us
    dot_general x1, matrix products, local(): lax.dot_general(pre_grad, fc1_weight, (((1,), (1,)), ((), ())), preferred...  20.2 us
    all_gather x1, blocking collectives, local(): lax.all_gather(merge_in, 'vit', axis=0, tiled=True)  16.7 us
    reduce_scatter x1, waiting for transfers between devices, local(): lax.psum_scatter(lax.dot_general(pre_grad, fc1_weight, (((1,), (1,)), (()...  14.3 us
    all_to_all x1, waiting for transfers between devices, local(): lax.all_to_all(projected, 'vit', split_axis=1, concat_axis=3, tiled=True)  11.3 us
    dot_general x1, matrix products, local(): jnp.dot(rows_in, fc1_weight, preferred_element_type=jnp.float32) + fc1_bias  9.08 us
  transfers between devices with their start and end apart: 6, of which 4 were waited for; matrix products, arithmetic and copies ran while one was open for 7% of the time, Pallas kernels for 0%

commit v1 on v0

--- a/solution.py
+++ b/solution.py
@@ -189,7 +189,12 @@
         head_inputs[0], head_inputs[1], head_inputs[2], head_grad[0]
     )
     head_result = jnp.stack([query_all, key_all, value_all])
-    returned = lax.all_to_all(head_result, "vit", split_axis=3, concat_axis=1, tiled=True)
+    returned = jnp.concatenate(
+        lax.all_to_all(
+            jnp.stack(jnp.split(head_result, lax.axis_size("vit"), axis=3)), "vit", 0, 0
+        ),
+        axis=1,
+    )
     projected_grad = returned.reshape(3 * vit_width, patches)
     normed_grad = lax.dot_general(
         projected_grad, qkv_full, (((0,), (1,)), ((), ())), preferred_element_type=jnp.float32

time: 351 us -> 337 us (0.960)
  blocking collectives: 46.3 us -> 38 us
  local copies, waits for them, and re-layouts: 13.8 us -> 9.03 us
    all_to_all x1, blocking collectives: 22.2 us -> 13.9 us  [local(): lax.all_to_all(jnp.stack(jnp.split(head_result, lax.axis_size('vit'), axi...]
where the time goes in v1:
time: 337 us; the launch traced here: 336 us
  waiting for transfers between devices  203 us (60%)
  matrix products  51.8 us (15%)
  blocking collectives  38 us (11%)
  between operations  15.2 us (5%)
  starting transfers between devices  14.8 us (4%)
  local copies, waits for them, and re-layouts  9.03 us (3%)
  other arithmetic  4.95 us (1%)
    all_gather x1, waiting for transfers between devices, local(): lax.all_gather(qkv_weight, 'section', axis=0, tiled=True)  136 us
    all_gather x1, waiting for transfers between devices, local(): lax.all_gather(proj_weight, 'section', axis=0, tiled=True)  40.3 us
    dot_general x1, matrix products, local(): lax.dot_general(pre_grad, fc1_weight, (((1,), (1,)), ((), ())), preferred...  20.2 us
    all_gather x1, blocking collectives, local(): lax.all_gather(merge_in, 'vit', axis=0, tiled=True)  16.7 us
    reduce_scatter x1, waiting for transfers between devices, local(): lax.psum_scatter(lax.dot_general(pre_grad, fc1_weight, (((1,), (1,)), (()...  14.3 us
    all_to_all x1, blocking collectives, local(): lax.all_to_all(jnp.stack(jnp.split(head_result, lax.axis_size('vit'), axi...  13.9 us
    all_to_all x1, waiting for transfers between devices, local(): lax.all_to_all(projected, 'vit', split_axis=1, concat_axis=3, tiled=True)  11.3 us
    dot_general x1, matrix products, local(): jnp.dot(rows_in, fc1_weight, preferred_element_type=jnp.float32) + fc1_bias  9.08 us
  transfers between devices with their start and end apart: 6, of which 4 were waited for; matrix products, arithmetic and copies ran while one was open for 7% of the time, Pallas kernels for 0%

profile of v1, /device:TPU:0, one launch (start us, length us, event | category | flops | bytes accessed | tf_op | source)
XLA Modules:
  0.0 336.3 jit_solution(12052647936396391410)
XLA Ops:
  7.4 7.4 %all-to-all-start = ((bf16[8,16,4096]{2,1,0:T(8,128)(2,1)}), bf16[8,16,4096]{2,1,0:T(8,128)(2,1)S(1)}, u32[]{:S(2)}, u32[]{:S(2)}) async-start(bf16[8,16,4096]{2,1,0:T(8,128)(2,1)} %bitcast.71), calls=%async_computation | async-start | bytes 2097152 | tf_op jit(solution)/shard_map/all_to_all | solution.py:80
  14.9 0.2 dynamic-slice_reduce_fusion
  15.1 0.2 reduce-window.4
  15.3 0.6 slice.17
  16.0 0.2 fusion.41
  16.3 0.2 fusion.36
  16.6 0.7 add_compare_fusion
  17.3 0.2 reshape.193
  17.5 16.7 %all_gather.13 = bf16[64,4608]{1,0:T(8,128)(2,1)S(1)} all-gather(bf16[32,4608]{1,0:T(8,128)(2,1)S(1)} %reshape.193), channel_id=1, replica_groups=mesh['section'=4,'vit'=2,'dp'=4] {'vit'}, dimensions={0}, use_global_device_ids=true | all-gather | bytes 884736 | tf_op jit(solution)/shard_map/all_gather | solution.py:95
  34.2 9.1 %convolution_add_fusion = f32[64,2304]{1,0:T(8,128)S(1)} fusion(bf16[64,4608]{1,0:T(8,128)(2,1)S(1)} %all_gather.13, bf16[4608,2304]{1,0:T(8,128)(2,1)} %param.27, f32[2304]{0:T(1024)S(1)} %copy-done.7), kind=kOutput, calls=%fused_computation.6 | convolution fusion | flops 1359101952 | bytes 22422528 | tf_op jit(solution)/shard_map/dot_general | solution.py:98
  43.3 0.3 fusion.6
  43.6 1.0 scatter_custom_fusion
  44.7 7.5 %all_gather.12 = bf16[64,4096]{1,0:T(8,128)(2,1)S(1)} all-gather(bf16[32,4096]{1,0:T(8,128)(2,1)S(1)} %select_convert_fusion), channel_id=1, replica_groups=mesh['section'=4,'vit'=2,'dp'=4] {'vit'}, dimensions={0}, use_global_device_ids=true | all-gather | bytes 786432 | tf_op jit(solution)/shard_map/all_gather | solution.py:96
  52.2 20.2 %convolution_convert_fusion = bf16[64,4608]{1,0:T(8,128)(2,1)} fusion(bf16[4608,2304]{1,0:T(8,128)(2,1)} %param.27, bf16[64,4096]{1,0:T(8,128)(2,1)S(1)} %all_gather.12, bf16[2304,4096]{1,0:T(8,128)(2,1)} %param.29, f32[64,2304]{1,0:T(8,128)S(1)} %convolution_add_fusion), kind=kOutput, calls=%fused_computation.2 | convolution fusion | flops 2568683520 | bytes 41811968 | tf_op jit(solution)/shard_map/dot_general | solution.py:104
  72.4 0.5 all-gather.5.cloned.1.call-update
  73.0 0.5 all-gather.3.cloned.1.call-update
  73.5 0.7 broadcast_compare_fusion
  74.3 0.2 fusion.34
  74.6 14.3 %reduce-scatter.2.cloned.1.call-done = bf16[32,4608]{1,0:T(8,128)(2,1)} async-done(((bf16[64,4608]{1,0:T(8,128)(2,1)}), bf16[32,4608]{1,0:T(8,128)(2,1)}) %reduce-scatter.2.cloned.1.call-update) | async-done | bytes 294928 | tf_op jit(solution)/shard_map/reduce_scatter | solution.py:103
  88.9 1.1 reshape.203
  90.0 0.2 multiply_reduce_fusion
  90.3 40.3 %all-gather.5.cloned.1.call-done = bf16[1152,1152]{1,0:T(8,128)(2,1)} async-done(((bf16[288,1152]{1,0:T(8,128)(2,1)}), bf16[1152,1152]{1,0:T(8,128)(2,1)}) %all-gather.5.cloned.1.call-update) | async-done | bytes 2654224 | tf_op jit(solution)/shard_map/all_gather | solution.py:63
  130.6 2.7 fusion.3
  133.3 0.9 copy.42
  134.2 3.5 %all-to-all-start.2 = ((bf16[1,16,72,128]{3,2,0,1:T(8,128)(2,1)}), bf16[1,16,72,128]{3,2,0,1:T(8,128)(2,1)S(1)}, u32[]{:S(2)}, u32[]{:S(2)}) async-start(bf16[1,16,72,128]{3,2,0,1:T(8,128)(2,1)} %bitcast.12), calls=%async_computation.3 | async-start | bytes 589824 | tf_op jit(solution)/shard_map/all_to_all | solution.py:120
  137.7 135.5 %all-gather.3.cloned.1.call-done = bf16[1152,3456]{1,0:T(8,128)(2,1)} async-done(((bf16[288,3456]{1,0:T(8,128)(2,1)}), bf16[1152,3456]{1,0:T(8,128)(2,1)}) %all-gather.3.cloned.1.call-update) | async-done | bytes 7962640 | tf_op jit(solution)/shard_map/all_gather | solution.py:62
  273.2 4.7 %fusion.1 = bf16[3456,128]{0,1:T(8,128)(2,1)S(1)} fusion(bf16[1152,3456]{1,0:T(8,128)(2,1)} %all-gather.3.cloned.1.call-done, bf16[128,1152]{1,0:T(8,128)(2,1)S(1)} %copy-done.3, f32[1152]{0:T(1024)S(1)} %copy-done.8, f32[1152]{0:T(1024)S(1)} %copy-done.6, f32[128]{0:T(128)S(1)} %add_rsqrt_fusion, f32[128]{0:T(128)S(1)} %broadcast_multiply_fusion.2), kind=kOutput, calls=%fused_computation.4 | convolution fusion | flops 1020542976 | bytes 9152512 | tf_op jit(solution)/shard_map/dot_general | solution.py:67
  278.0 1.0 copy.39
  279.0 1.1 copy.40
  280.1 3.7 %all-to-all-start.1 = ((bf16[3,16,72,128]{3,2,0,1:T(8,128)(2,1)}), bf16[3,16,72,128]{3,2,0,1:T(8,128)(2,1)S(1)}, u32[]{:S(2)}, u32[]{:S(2)}) async-start(bf16[3,16,72,128]{3,2,0,1:T(8,128)(2,1)} %copy.40), calls=%async_computation.2 | async-start | bytes 1769472 | tf_op jit(solution)/shard_map/all_to_all | solution.py:119
  284.0 0.3 copy.55
  284.4 0.2 reshape.200
  284.6 11.3 %all-to-all-done.1 = bf16[3,16,72,128]{3,2,0,1:T(8,128)(2,1)S(1)} async-done(((bf16[3,16,72,128]{3,2,0,1:T(8,128)(2,1)}), bf16[3,16,72,128]{3,2,0,1:T(8,128)(2,1)S(1)}, u32[]{:S(2)}, u32[]{:S(2)}) %all-to-all-start.1) | async-done | bytes 884768 | tf_op jit(solution)/shard_map/all_to_all | solution.py:119
  295.9 0.9 copy.54
  296.8 0.6 fusion.62
  297.4 0.2 reshape.199
  297.6 0.2 squeeze.21
  297.8 0.2 squeeze.24
  298.0 0.7 fusion.63
  298.8 0.2 divide_convert_fusion
  299.0 0.4 fusion.14
  299.4 1.9 fusion.64
  301.3 3.0 fusion.12
  304.3 3.1 fusion.13
  307.5 0.2 slice_bitcast_fusion.1
  307.8 13.9 %all_to_all.40 = bf16[2,3,8,72,128]{4,3,2,1,0:T(8,128)(2,1)S(1)} all-to-all(bf16[2,3,8,72,128]{4,3,2,1,0:T(8,128)(2,1)S(1)} %pad_maximum_fusion.1), channel_id=1, replica_groups=mesh['section'=4,'vit'=2,'dp'=4] {'vit'}, dimensions={0} | all-to-all | bytes 1769472 | tf_op jit(solution)/shard_map/all_to_all | solution.py:193
  321.7 6.0 %fusion.61 = (f32[128]{0:T(128)S(1)}, f32[128]{0:T(128)S(1)}, f32[128,1152]{1,0:T(8,128)S(1)}) fusion(f32[128]{0:T(128)S(1)} %add_rsqrt_fusion, f32[128]{0:T(128)S(1)} %broadcast_multiply_fusion.2, bf16[128,1152]{1,0:T(8,128)(2,1)S(1)} %copy-done.3, f32[1152]{0:T(1024)S(1)} %copy-done.6, bf16[3456,128]{1,0:T(8,128)(2,1)S(1)} %bitcast.64, ...), kind=kOutput, calls=%fused_computation.106 | convolution fusion | flops 1020247808 | bytes 9738752 | tf_op jit(solution)/shard_map/dot_general | solution.py:199
  327.7 1.1 fusion.33
  (51 shorter events, 1.2 us)
Async XLA Ops:
  7.4 7.5 %copy-start = (s32[4,2]{0,1:T(2,128)S(1)}, s32[4,2]{0,1:T(2,128)}, u32[]{:S(2)}) copy-start(s32[4,2]{0,1:T(2,128)} %param.17) | copy-start | bytes 100
  7.4 8.5 %copy-start.2 = (bf16[128,1152]{1,0:T(8,128)(2,1)S(1)}, bf16[128,1152]{1,0:T(8,128)(2,1)}, u32[]{:S(2)}) copy-start(bf16[128,1152]{1,0:T(8,128)(2,1)} %param.20) | copy-start | bytes 884740
  7.4 8.8 %copy-start.10 = (s32[2,128]{1,0:T(2,128)S(1)}, s32[2,128]{1,0:T(2,128)}, u32[]{:S(2)}) copy-start(s32[2,128]{1,0:T(2,128)} %param.16) | copy-start | bytes 3076
  7.4 8.9 %copy-start.9 = (f32[1152]{0:T(1024)S(1)}, f32[1152]{0:T(1024)}, u32[]{:S(2)}) copy-start(f32[1152]{0:T(1024)} %param.26) | copy-start | bytes 13828
  7.4 8.9 %copy-start.5 = (f32[1152]{0:T(1024)S(1)}, f32[1152]{0:T(1024)}, u32[]{:S(2)}) copy-start(f32[1152]{0:T(1024)} %param.25) | copy-start | bytes 13828
  7.4 26.8 %copy-start.11 = (s32[4]{0:T(128)S(1)}, s32[4]{0:T(128)}, u32[]{:S(2)}) copy-start(s32[4]{0:T(128)} %param.18) | copy-start | bytes 52
  7.4 26.8 %copy-start.7 = (f32[2304]{0:T(1024)S(1)}, f32[2304]{0:T(1024)}, u32[]{:S(2)}) copy-start(f32[2304]{0:T(1024)} %param.28) | copy-start | bytes 27652
  7.4 35.8 %all-to-all-start = ((bf16[8,16,4096]{2,1,0:T(8,128)(2,1)}), bf16[8,16,4096]{2,1,0:T(8,128)(2,1)S(1)}, u32[]{:S(2)}, u32[]{:S(2)}) async-start(bf16[8,16,4096]{2,1,0:T(8,128)(2,1)} %bitcast.71), calls=%async_computation | async-start | bytes 2097152 | tf_op jit(solution)/shard_map/all_to_all | solution.py:80
  14.8 74.0 %reduce-scatter.2.cloned.1.call-start = ((), (), s32[]{:S(2)}) async-start(), calls=%async_computation.5 | async-start | bytes 884736 | tf_op jit(solution)/shard_map/reduce_scatter | solution.py:103
  72.3 1.9 copy-start.3
  72.4 58.2 %all-gather.5.cloned.1.call-start = ((), (), s32[]{:S(2)}) async-start(), calls=%async_computation.7 | async-start | bytes 3317760 | tf_op jit(solution)/shard_map/all_gather | solution.py:63
  72.9 200.3 %all-gather.3.cloned.1.call-start = ((), (), s32[]{:S(2)}) async-start(), calls=%async_computation.6 | async-start | bytes 9953280 | tf_op jit(solution)/shard_map/all_gather | solution.py:62
  130.6 142.6 %copy-start.6 = (f32[1152]{0:T(1024)S(1)}, f32[1152]{0:T(1024)}, u32[]{:S(2)}) copy-start(f32[1152]{0:T(1024)} %param.21) | copy-start | bytes 13828
  130.6 142.6 %copy-start.8 = (f32[1152]{0:T(1024)S(1)}, f32[1152]{0:T(1024)}, u32[]{:S(2)}) copy-start(f32[1152]{0:T(1024)} %param.22) | copy-start | bytes 13828
  134.2 145.8 %all-to-all-start.2 = ((bf16[1,16,72,128]{3,2,0,1:T(8,128)(2,1)}), bf16[1,16,72,128]{3,2,0,1:T(8,128)(2,1)S(1)}, u32[]{:S(2)}, u32[]{:S(2)}) async-start(bf16[1,16,72,128]{3,2,0,1:T(8,128)(2,1)} %bitcast.12), calls=%async_computation.3 | async-start | bytes 589824 | tf_op jit(solution)/shard_map/all_to_all | solution.py:120
  280.1 15.8 %all-to-all-start.1 = ((bf16[3,16,72,128]{3,2,0,1:T(8,128)(2,1)}), bf16[3,16,72,128]{3,2,0,1:T(8,128)(2,1)S(1)}, u32[]{:S(2)}, u32[]{:S(2)}) async-start(bf16[3,16,72,128]{3,2,0,1:T(8,128)(2,1)} %copy.40), calls=%async_computation.2 | async-start | bytes 1769472 | tf_op jit(solution)/shard_map/all_to_all | solution.py:119
  297.8 0.9 copy-start.4
  321.7 7.2 %copy-start.1 = (s32[4,2]{0,1:T(2,128)S(1)}, s32[4,2]{0,1:T(2,128)}, u32[]{:S(2)}) copy-start(s32[4,2]{0,1:T(2,128)} %param.17) | copy-start | bytes 100
Sparse Core Ops, SparseCore 0:
  72.5 16.3 reduce-scatter.1
Sparse Core Ops, SparseCore 1:
  74.4 56.1 all-gather.4
  132.1 141.1 all-gather.2
